TPU v7x, 32 devices: a whole 2x2x4 slice. The times are simulated.
32 devices in a mesh: row: 4 (over z), col: 2 (over x), rep: 4 (over y, core).
Axes of the slice: x: 2, y: 2, z: 4, core: 2. Of those that a mesh axis runs over, the one named last changes fastest.
Arguments:
- features: bfloat16 [8192, 256], P(('col', 'rep'), 'row'), may hold values from -6 to 6
- weight: bfloat16 [256, 256], replicated, may hold values from -0.375 to 0.375
- cotangent: bfloat16 [8192, 256], P(('row', 'col', 'rep')), may hold values from -6 to 6
- block_values: bfloat16 [4, 8, 128, 128, 128], P('row', ('col', 'rep')), may hold values from -0.0625 to 0.0625
- block_coords: int32 [4, 8, 128, 2], P('row', ('col', 'rep')), may hold values from 0 to 15, as said below
- block_counts: int32 [4, 8], P('row', ('col', 'rep')), may hold values from 1 to 128, as said below
Outputs:
- activations: bfloat16 [8192, 256], P(('row', 'col', 'rep'))
- input_grad: bfloat16 [8192, 256], P(('col', 'rep'), 'row')
- weight_grad: float32 [256, 256], replicated
Inputs may be any that keep to these rules, and one draw needn't show every extreme that they name: `block_coords`: each slot's row block is below 16 and its column block below 8. `block_counts`: some tile uses all 128 slots.
All inputs are finite; a program needn't handle non-finite values.
Results may differ from a plain program's by a relative error of at most 0.014.
Values may be sent and summed in bfloat16 or wider, within the bound.
A program may use at most 128 MiB of HBM per device.

v0:
```python
import functools
import math

import jax
import jax.numpy as jnp
from jax import lax
from jax.experimental import pallas as pl
from jax.experimental.pallas import tpu as pltpu
from jax.sharding import PartitionSpec as P


def local_xla(features, weight, cotangent, block_values, block_coords, block_counts):
    blocks = block_values[0, 0]
    coords = block_coords[0, 0]
    live_count = block_counts[0, 0]
    slots = blocks.shape[0]
    gathered = lax.all_gather(features, "row", axis=1, tiled=True)
    feat_width = gathered.shape[1]
    col_blocks = gathered.shape[0] // 128
    row_blocks = cotangent.shape[0] * lax.axis_size(("col", "rep")) // 128
    feat_blocks = gathered.reshape(col_blocks, 128, feat_width)
    is_live = (jnp.arange(slots, dtype=jnp.int32) < live_count).astype(jnp.float32)
    per_turn = math.gcd(slots, 64)
    rounds = slots // per_turn
    pieces = (
        blocks.reshape(rounds, per_turn, 128, 128),
        coords[:, 0].reshape(rounds, per_turn),
        coords[:, 1].reshape(rounds, per_turn),
        is_live.reshape(rounds, per_turn),
    )

    def forward_step(total, piece):
        blocks_g, rows_g, cols_g, live_g = piece
        chosen = feat_blocks[cols_g]
        product = jnp.einsum("bij,bjf->bif", blocks_g, chosen, preferred_element_type=jnp.float32)
        return (total.at[rows_g].add(product * live_g[:, None, None]), None)

    partial_value, _ = lax.scan(
        forward_step, jnp.zeros((row_blocks, 128, feat_width), jnp.float32), pieces
    )
    partial_value = partial_value.reshape(row_blocks * 128, feat_width)
    summed = lax.psum_scatter(partial_value, ("col", "rep"), scatter_dimension=0, tiled=True)
    aggregate = summed.astype(jnp.bfloat16)
    pre_act = jnp.dot(aggregate, weight, preferred_element_type=jnp.float32)
    sigma = jax.nn.sigmoid(pre_act)
    activations = (pre_act * sigma).astype(jnp.bfloat16)
    grad_pre = (cotangent.astype(jnp.float32) * sigma * (1.0 + pre_act * (1.0 - sigma))).astype(
        jnp.bfloat16
    )
    weight_terms = jnp.dot(aggregate.T, grad_pre, preferred_element_type=jnp.float32)
    share = lax.psum_scatter(
        weight_terms.astype(jnp.bfloat16), ("col", "rep"), scatter_dimension=0, tiled=True
    ).astype(jnp.float32)
    share = lax.psum(share, "row")
    weight_grad = lax.all_gather(share, ("col", "rep"), axis=0, tiled=True)
    back_rows = jnp.dot(grad_pre, weight.T, preferred_element_type=jnp.float32).astype(jnp.bfloat16)
    back_all = lax.all_gather(back_rows, ("col", "rep"), axis=0, tiled=True)
    back_blocks = back_all.reshape(row_blocks, 128, back_all.shape[1])

    def backward_step(total, piece):
        blocks_g, rows_g, cols_g, live_g = piece
        chosen = back_blocks[rows_g]
        product = jnp.einsum("bji,bjf->bif", blocks_g, chosen, preferred_element_type=jnp.float32)
        return (total.at[cols_g].add(product * live_g[:, None, None]), None)

    grad_terms, _ = lax.scan(
        backward_step, jnp.zeros((col_blocks, 128, back_all.shape[1]), jnp.float32), pieces
    )
    grad_terms = grad_terms.reshape(col_blocks * 128, back_all.shape[1])
    input_grad = lax.psum_scatter(
        grad_terms.astype(jnp.bfloat16), "row", scatter_dimension=1, tiled=True
    )
    return (activations, input_grad, weight_grad)


BF16 = jnp.bfloat16
F32 = jnp.float32
VMEM_BUDGET = 60 * 2**20
MESH = pl.DeviceIdType.MESH


def dot(a, b, ca=1, cb=0):
    return lax.dot_general(a, b, (((ca,), (cb,)), ((), ())), preferred_element_type=F32)


def layer_kernel(
    sizes,
    count_in,
    coords_in,
    feat_in,
    weight_in,
    cot_in,
    blocks_hbm,
    act_out,
    igrad_out,
    wgrad_out,
    fbuf,
    bbuf,
    sums,
    dense,
    feat,
    pbuf,
    prec,
    qbuf,
    qrec,
    own_back,
    brec,
    bpar,
    total,
    zbuf,
    zrec,
    wbuf,
    wrec,
    shard_buf,
    srec,
    wall,
    tvec,
    table,
    load_sem,
    t_sem,
    f_sem,
    p_sem,
    q_sem,
    b_sem,
    c_sem,
    z_sem,
    w_sem,
    s_sem,
    g_sem,
):
    nrow, ncol, nrep = sizes
    nh = nrep // 2
    group = ncol * nrep
    slots = bbuf.shape[0]
    nodes, width = act_out.shape
    fw, col_nodes = feat_in.shape
    row_blocks, col_blocks = dense.shape[0] // 128, dense.shape[1] // 128
    r, c, p = lax.axis_index("row"), lax.axis_index("col"), lax.axis_index("rep")
    h, k = p // 2, p % 2
    g = c * nrep + p
    partner = h * 2 + (1 - k)
    offsets = [(dc, dh) for dc in reversed(range(ncol)) for dh in reversed(range(nh))]
    chips = len(offsets)

    def to_row(j):
        return {"row": (r + j) % nrow}

    def to_group(j):
        q = (g + j) % group
        return {"col": q // nrep, "rep": q % nrep}

    def to_chip(i):
        dc, dh = offsets[i]
        return {"col": (c + dc) % ncol, "rep": ((h + dh) % nh) * 2 + k}

    def part_to(i, core):
        dc, dh = offsets[i]
        return ((c + dc) % ncol) * nrep + ((h + dh) % nh) * 2 + core

    def part_from(i, core):
        dc, dh = offsets[i]
        return ((c + ncol - dc) % ncol) * nrep + ((h + nh - dh) % nh) * 2 + core

    def nearest(n):
        code = 0
        for q in range(nrow):
            order = sorted(range(nrow), key=lambda t: (abs(t - q), t))
            code += order[n] * nrow**q
        power = 1
        for q in range(1, nrow):
            power = power * jnp.where(r >= q, nrow, 1)
        return (code // power) % nrow

    def rcopy(src, dst, sems, i, device):
        return pltpu.make_async_remote_copy(
            src_ref=src,
            dst_ref=dst,
            send_sem=sems.at[0, i],
            recv_sem=sems.at[1, i],
            device_id=device,
            device_id_type=MESH,
        )

    chunks = load_sem.shape[0]
    per = slots // chunks
    loads = []
    for i in range(chunks):
        span = pl.ds(i * per, per)
        loads.append(pltpu.make_async_copy(blocks_hbm.at[span], bbuf.at[span], load_sem.at[i]))
        loads[-1].start()

    barrier = pltpu.get_barrier_semaphore()
    for j in range(1, nrow):
        pl.semaphore_signal(barrier, inc=1, device_id=to_row(j), device_id_type=MESH)
    for j in range(1, group):
        pl.semaphore_signal(barrier, inc=1, device_id=to_group(j), device_id_type=MESH)

    pl.semaphore_wait(barrier, nrow - 1 + group - 1)
    fcopies = []
    for side in range(2):
        there = r > 0 if side == 0 else r < nrow - 1
        copy = rcopy(feat_in, fbuf.at[r], f_sem.at[side], r, {"row": (r + nrow - 1 + 2 * side) % nrow})
        fcopies.append((there, copy))

        @pl.when(there)
        def _(copy=copy):
            copy.start()

    fbuf[r] = feat_in[...]

    places = row_blocks * col_blocks
    live = count_in[0, 0]
    row_form = coords_in[0:1, :] * col_blocks + coords_in[1:2, :]
    column_form = jnp.broadcast_to(row_form, (slots, slots)).T
    mine_at = lax.broadcasted_iota(jnp.int32, (slots, slots), 0)
    other_at = lax.broadcasted_iota(jnp.int32, (slots, slots), 1)
    hit = (column_form == row_form) & (mine_at < jnp.minimum(other_at, live))
    tvec[0:1, 0:slots] = jnp.max(jnp.where(hit, mine_at + 1, 0), axis=0, keepdims=True)
    for start in range(0, places, slots):
        hit = (column_form == other_at + start) & (mine_at < live)
        tvec[0:1, slots + start : 2 * slots + start] = jnp.max(
            jnp.where(hit, mine_at + 1, 0), axis=0, keepdims=True
        )
    tcopy = pltpu.make_async_copy(tvec, table, t_sem)
    tcopy.start()
    tcopy.wait()

    sums[0] = jnp.zeros((128, 128), F32)
    for i in range(chunks):
        loads[i].wait()

        def add_slot(s, carry):
            sums[s + 1] = sums[table[0, s]] + bbuf[s].astype(F32)
            return carry

        lax.fori_loop(i * per, (i + 1) * per, add_slot, 0)

    def fill(rb, carry):
        for cb in range(col_blocks):
            block = sums[table[0, slots + rb * col_blocks + cb]]
            dense[pl.ds(rb * 128, 128), cb * 128 : (cb + 1) * 128] = block.astype(BF16)
        return carry

    lax.fori_loop(0, row_blocks, fill, 0)

    half = nodes // 2

    def partial(part, slot):
        x = dot(dense[pl.ds(part * nodes, nodes), :], fbuf[slot], 1, 1)
        return jnp.concatenate([x[:half], x[half:]], axis=1)

    qcopies = []

    def merge(n, pcopy, mine):
        pcopy.wait()
        for i in range(chips - 1):
            qbuf[n, i] = (mine[i] + prec[n, i].astype(F32)).astype(BF16)
            copy = rcopy(qbuf.at[n, i], qrec.at[n, i], q_sem.at[n], i, to_chip(i))
            copy.start()
            qcopies.append(copy)
        return mine[chips - 1] + prec[n, chips - 1].astype(F32)

    held, waiting = [], None
    for n in range(nrow):
        slot = nearest(n)
        if n > 0:
            side = (slot < r).astype(jnp.int32)
            there = jnp.where(slot < r, r < nrow - 1, r > 0)
            copy = rcopy(
                fbuf.at[slot], fbuf.at[slot], f_sem.at[side], slot, {"row": (r + nrow - 1 + 2 * side) % nrow}
            )
            copy.wait_recv()
            fcopies.append((there, copy))

            @pl.when(there)
            def _(copy=copy):
                copy.start()

        for i in range(chips):
            pbuf[n, i] = partial(part_to(i, 1 - k), slot).astype(BF16)
        pcopy = rcopy(pbuf.at[n], prec.at[n], p_sem, n, {"rep": partner})
        pcopy.start()
        if waiting is not None:
            held.append(merge(*waiting))
        waiting = (n, pcopy, [partial(part_to(i, k), slot) for i in range(chips)])
    held.append(merge(*waiting))
    for there, copy in fcopies:

        @pl.when(there)
        def _(copy=copy):
            copy.wait_send()

    for n in range(nrow):
        got = held[n]
        for i in range(chips - 1):
            qcopies[n * (chips - 1) + i].wait()
            got = got + qrec[n, i].astype(F32)
        feat[nearest(n)] = got.astype(BF16)

    spread = jnp.concatenate([feat[m] for m in range(nrow)], axis=1)
    pieces = [spread[:, m * fw : (m + 1) * fw] for m in range(2 * nrow)]
    aggregate = jnp.concatenate(
        [jnp.concatenate(pieces[0::2], axis=1), jnp.concatenate(pieces[1::2], axis=1)], axis=0
    )
    pre_act = dot(aggregate, weight_in[...])
    sigma = jax.nn.sigmoid(pre_act)
    grad_pre = (cot_in[...].astype(F32) * sigma * (1.0 + pre_act * (1.0 - sigma))).astype(BF16)
    own_back[...] = dot(weight_in[...], grad_pre, 1, 1).astype(BF16)
    bcopies, ccopies = [], []
    for i in range(chips - 1):
        bcopies.append(rcopy(own_back, brec.at[i], b_sem, i, to_chip(i)))
        bcopies[i].start()
    first = rcopy(own_back, bpar.at[chips - 1], c_sem, chips - 1, {"rep": partner})
    first.start()

    terms = dot(aggregate, grad_pre, 0, 0)
    srows = width // group
    wbuf[...] = terms.astype(BF16).reshape(group, srows, width)
    wcopies = []
    for j in range(1, group):
        wcopies.append(rcopy(wbuf.at[(g + j) % group], wrec.at[j - 1], w_sem, j - 1, to_group(j)))
        wcopies[-1].start()
    act_out[...] = (pre_act * sigma).astype(BF16)

    def back_term(piece_t, part):
        return dot(piece_t, dense[pl.ds(part * nodes, nodes), :])

    total[...] = back_term(own_back[...], g)
    first.wait()
    total[...] += back_term(bpar[chips - 1], c * nrep + partner)

    for i in reversed(range(chips - 1)):
        bcopies[i].wait()
        ccopies.append(rcopy(brec.at[i], bpar.at[i], c_sem, i, {"rep": partner}))
        ccopies[-1].start()
        total[...] += back_term(brec[i], part_from(i, k))

    share = wbuf[g].astype(F32)
    for j in range(group - 1):
        wcopies[j].wait()
        share = share + wrec[j].astype(F32)
    shard_buf[...] = share.astype(BF16)
    scopies = []
    for j in range(1, nrow):
        scopies.append(rcopy(shard_buf, srec.at[j - 1], s_sem, j - 1, to_row(j)))
        scopies[-1].start()

    for n, i in enumerate(reversed(range(chips - 1))):
        ccopies[n].wait()
        total[...] += back_term(bpar[i], part_from(i, 1 - k))

    zcopies = []
    for j in range(1, nrow):
        q = (r + j) % nrow
        zbuf[j - 1] = total[pl.ds(q * fw, fw), :].astype(BF16)
        zcopies.append(rcopy(zbuf.at[j - 1], zrec.at[j - 1], z_sem, j - 1, to_row(j)))
        zcopies[-1].start()

    for j in range(nrow - 1):
        scopies[j].wait()
        share = share + srec[j].astype(F32)
    wall[g] = share
    gcopies = []
    for j in range(1, group):
        gcopies.append(rcopy(wall.at[g], wall.at[g], g_sem, j - 1, to_group(j)))
        gcopies[-1].start()

    mine = total[pl.ds(r * fw, fw), :]
    for j in range(nrow - 1):
        zcopies[j].wait()
        mine = mine + zrec[j].astype(F32)
    igrad_out[...] = mine.astype(BF16)
    for copy in gcopies:
        copy.wait()
    wgrad_out[...] = wall[...].reshape(width, width)


def keep_kernel(a_in, b_in, c_in, a_out, b_out, c_out):
    a_out[...] = a_in[...]
    b_out[...] = b_in[...]
    c_out[...] = c_in[...]


def local_kernel(sizes, features, weight, cotangent, block_values, block_coords, block_counts):
    nrow, ncol, nrep = sizes
    group = ncol * nrep
    chips = group // 2
    blocks = block_values[0, 0]
    slots = blocks.shape[0]
    nodes, width = cotangent.shape
    col_nodes, fw = features.shape
    row_blocks = nodes * group // 128
    places = row_blocks * (col_nodes // 128)
    chunks = math.gcd(slots, 8)
    srows = width // group
    square = (nodes, width)
    half = (nodes // 2, 2 * fw)
    vmem = functools.partial(pl.BlockSpec, memory_space=pltpu.VMEM)
    dma = pltpu.SemaphoreType.DMA
    outs = pl.pallas_call(
        functools.partial(layer_kernel, sizes),
        out_shape=(
            jax.ShapeDtypeStruct(square, BF16),
            jax.ShapeDtypeStruct((fw, col_nodes), BF16),
            jax.ShapeDtypeStruct((width, width), F32),
        ),
        in_specs=[
            pl.BlockSpec(memory_space=pltpu.SMEM),
            vmem(),
            vmem(),
            vmem(),
            vmem(),
            pl.BlockSpec(memory_space=pl.ANY),
        ],
        out_specs=(vmem(), vmem(), vmem()),
        scratch_shapes=[
            pltpu.VMEM((nrow, fw, col_nodes), BF16),
            pltpu.VMEM((slots, 128, 128), BF16),
            pltpu.VMEM((slots + 1, 128, 128), F32),
            pltpu.VMEM((row_blocks * 128, col_nodes), BF16),
            pltpu.VMEM((nrow,) + half, BF16),
            pltpu.VMEM((nrow, chips) + half, BF16),
            pltpu.VMEM((nrow, chips) + half, BF16),
            pltpu.VMEM((nrow, chips - 1) + half, BF16),
            pltpu.VMEM((nrow, chips - 1) + half, BF16),
            pltpu.VMEM((width, nodes), BF16),
            pltpu.VMEM((chips - 1, width, nodes), BF16),
            pltpu.VMEM((chips, width, nodes), BF16),
            pltpu.VMEM((width, col_nodes), F32),
            pltpu.VMEM((nrow - 1, fw, col_nodes), BF16),
            pltpu.VMEM((nrow - 1, fw, col_nodes), BF16),
            pltpu.VMEM((group, srows, width), BF16),
            pltpu.VMEM((group - 1, srows, width), BF16),
            pltpu.VMEM((srows, width), BF16),
            pltpu.VMEM((nrow - 1, srows, width), BF16),
            pltpu.VMEM((group, srows, width), F32),
            pltpu.VMEM((1, slots + places), jnp.int32),
            pltpu.SMEM((1, slots + places), jnp.int32),
            dma((chunks,)),
            dma,
            dma((2, 2, nrow)),
            dma((2, nrow)),
            dma((nrow, 2, chips - 1)),
            dma((2, chips - 1)),
            dma((2, chips)),
            dma((2, nrow - 1)),
            dma((2, group - 1)),
            dma((2, nrow - 1)),
            dma((2, group - 1)),
        ],
        compiler_params=pltpu.CompilerParams(
            collective_id=0, has_side_effects=True, vmem_limit_bytes=VMEM_BUDGET
        ),
    )(block_counts, block_coords[0, 0].T, features.T, weight, cotangent, blocks)
    activations, input_grad_t, weight_grad = pl.pallas_call(
        keep_kernel,
        out_shape=tuple(jax.ShapeDtypeStruct(x.shape, x.dtype) for x in outs),
        in_specs=[vmem()] * 3,
        out_specs=(vmem(),) * 3,
    )(*outs)
    return activations, input_grad_t.T, weight_grad


def fits(mesh, features, weight, cotangent, block_values):
    nrow, ncol, nrep = (mesh.shape[name] for name in ("row", "col", "rep"))
    group = ncol * nrep
    width = features.shape[1]
    fw = width // nrow
    rows, cols = cotangent.shape[0] // nrow, features.shape[0] // group
    tile = rows * cols * 2 + block_values.shape[2] * 128 * 128 * 6
    moved = 8 * rows * width + 12 * cols * width
    whole = nrep % 2 == 0 and block_values.shape[2] == 128 and rows * cols % 128**3 == 0
    whole = whole and 2 * fw == 128 and width % (16 * group) == 0
    return whole and nrow > 1 and group > 2 and tile + moved < VMEM_BUDGET * 3 // 4


def solution(mesh):
    in_specs = (
        P(("col", "rep"), "row"),
        P(),
        P(("row", "col", "rep"), None),
        P("row", ("col", "rep"), None, None, None),
        P("row", ("col", "rep"), None, None),
        P("row", ("col", "rep")),
    )
    out_specs = (P(("row", "col", "rep"), None), P(("col", "rep"), "row"), P())
    sizes = tuple(mesh.shape[name] for name in ("row", "col", "rep"))

    def run(features, weight, cotangent, block_values, block_coords, block_counts):
        if fits(mesh, features, weight, cotangent, block_values):
            body = functools.partial(local_kernel, sizes)
        else:
            body = local_xla
        return jax.shard_map(
            body, mesh=mesh, in_specs=in_specs, out_specs=out_specs, check_vma=False
        )(features, weight, cotangent, block_values, block_coords, block_counts)

    return run
```

profile of v0, /device:TPU:0, one launch (start us, length us, event | category | flops | bytes accessed | tf_op | source)
XLA Modules:
  0.0 51.2 jit_solution(16584680417059395806)
XLA Ops:
  1.3 48.0 %shard_map.85 = (bf16[256,256]{1,0:T(8,128)(2,1)}, bf16[64,1024]{1,0:T(8,128)(2,1)}, f32[256,256]{1,0:T(8,128)}) custom-call(s32[1,1]{1,0:T(1,128)S(6)} %copy.9.count_in, s32[2,128]{1,0:T(2,128)} %bitcast.8, bf16[64,1024]{1,0:T(8,128)(2,1)} %bitcast.7, bf16[256,256]{1,0:T(8,128)(2,1)} %weight_in.1, bf16[256,256]{1,0:T(8,128)(2,1)} %cot_in.1, ...), custom_call_target="tpu_custom_call" | custom-call | tf_op jit(solution)/shard_map/pallas_call | solution.py:400
  49.3 1.9 %shard_map.86 = (bf16[256,256]{1,0:T(8,128)(2,1)}, bf16[64,1024]{1,0:T(8,128)(2,1)}, f32[256,256]{1,0:T(8,128)}) custom-call(bf16[256,256]{1,0:T(8,128)(2,1)} %get-tuple-element.9.a_in, bf16[64,1024]{1,0:T(8,128)(2,1)} %get-tuple-element.10.b_in, f32[256,256]{1,0:T(8,128)} %get-tuple-element.11.c_in), custom_call_target="tpu_custom_call" | custom-call | tf_op jit(solution)/shard_map/pallas_call | solution.py:455
where the time goes:
time: 51.3 us; the launch traced here: 51.2 us
  Pallas kernels  49.9 us (97%)
  between operations  1.29 us (3%)
    pallas_call x1, Pallas kernels, local_kernel(): pl.pallas_call(functools.partial(layer_kernel, sizes), out_shape=(jax.Sha...  48 us
    pallas_call x1, Pallas kernels, local_kernel(): pl.pallas_call(keep_kernel, out_shape=tuple((jax.ShapeDtypeStruct(x.shape...  1.88 us

commit v1 on v0

v1 whole, which is shorter than its diff:
```python
import functools
import math

import jax
import jax.numpy as jnp
from jax import lax
from jax.experimental import pallas as pl
from jax.experimental.pallas import tpu as pltpu
from jax.sharding import PartitionSpec as P


def local_xla(features, weight, cotangent, block_values, block_coords, block_counts):
    blocks = block_values[0, 0]
    coords = block_coords[0, 0]
    live_count = block_counts[0, 0]
    slots = blocks.shape[0]
    gathered = lax.all_gather(features, "row", axis=1, tiled=True)
    feat_width = gathered.shape[1]
    col_blocks = gathered.shape[0] // 128
    row_blocks = cotangent.shape[0] * lax.axis_size(("col", "rep")) // 128
    feat_blocks = gathered.reshape(col_blocks, 128, feat_width)
    is_live = (jnp.arange(slots, dtype=jnp.int32) < live_count).astype(jnp.float32)
    per_turn = math.gcd(slots, 64)
    rounds = slots // per_turn
    pieces = (
        blocks.reshape(rounds, per_turn, 128, 128),
        coords[:, 0].reshape(rounds, per_turn),
        coords[:, 1].reshape(rounds, per_turn),
        is_live.reshape(rounds, per_turn),
    )

    def forward_step(total, piece):
        blocks_g, rows_g, cols_g, live_g = piece
        chosen = feat_blocks[cols_g]
        product = jnp.einsum("bij,bjf->bif", blocks_g, chosen, preferred_element_type=jnp.float32)
        return (total.at[rows_g].add(product * live_g[:, None, None]), None)

    partial_value, _ = lax.scan(
        forward_step, jnp.zeros((row_blocks, 128, feat_width), jnp.float32), pieces
    )
    partial_value = partial_value.reshape(row_blocks * 128, feat_width)
    summed = lax.psum_scatter(partial_value, ("col", "rep"), scatter_dimension=0, tiled=True)
    aggregate = summed.astype(jnp.bfloat16)
    pre_act = jnp.dot(aggregate, weight, preferred_element_type=jnp.float32)
    sigma = jax.nn.sigmoid(pre_act)
    activations = (pre_act * sigma).astype(jnp.bfloat16)
    grad_pre = (cotangent.astype(jnp.float32) * sigma * (1.0 + pre_act * (1.0 - sigma))).astype(
        jnp.bfloat16
    )
    weight_terms = jnp.dot(aggregate.T, grad_pre, preferred_element_type=jnp.float32)
    share = lax.psum_scatter(
        weight_terms.astype(jnp.bfloat16), ("col", "rep"), scatter_dimension=0, tiled=True
    ).astype(jnp.float32)
    share = lax.psum(share, "row")
    weight_grad = lax.all_gather(share, ("col", "rep"), axis=0, tiled=True)
    back_rows = jnp.dot(grad_pre, weight.T, preferred_element_type=jnp.float32).astype(jnp.bfloat16)
    back_all = lax.all_gather(back_rows, ("col", "rep"), axis=0, tiled=True)
    back_blocks = back_all.reshape(row_blocks, 128, back_all.shape[1])

    def backward_step(total, piece):
        blocks_g, rows_g, cols_g, live_g = piece
        chosen = back_blocks[rows_g]
        product = jnp.einsum("bji,bjf->bif", blocks_g, chosen, preferred_element_type=jnp.float32)
        return (total.at[cols_g].add(product * live_g[:, None, None]), None)

    grad_terms, _ = lax.scan(
        backward_step, jnp.zeros((col_blocks, 128, back_all.shape[1]), jnp.float32), pieces
    )
    grad_terms = grad_terms.reshape(col_blocks * 128, back_all.shape[1])
    input_grad = lax.psum_scatter(
        grad_terms.astype(jnp.bfloat16), "row", scatter_dimension=1, tiled=True
    )
    return (activations, input_grad, weight_grad)


BF16 = jnp.bfloat16
F32 = jnp.float32
VMEM_BUDGET = 60 * 2**20
MESH = pl.DeviceIdType.MESH


def dot(a, b, ca=1, cb=0):
    return lax.dot_general(a, b, (((ca,), (cb,)), ((), ())), preferred_element_type=F32)


def layer_kernel(
    sizes,
    count_hbm,
    coords_hbm,
    feat_hbm,
    weight_hbm,
    cot_hbm,
    blocks_hbm,
    act_hbm,
    igrad_hbm,
    wgrad_hbm,
    act_out,
    igrad_out,
    wgrad_out,
    count_in,
    coords_in,
    weight_in,
    cot_in,
    fbuf,
    bbuf,
    sums,
    dense,
    pbuf,
    prec,
    ownp,
    qbuf,
    qrec,
    held,
    agg,
    own_back,
    bown,
    brec,
    bpar,
    total,
    zbuf,
    zrec,
    wbuf,
    wrec,
    wrow,
    wall,
    tvec,
    table,
    load_sem,
    in_sem,
    t_sem,
    f_sem,
    p_sem,
    q_sem,
    b_sem,
    o_sem,
    c_sem,
    z_sem,
    w_sem,
    s_sem,
    g_sem,
):
    nrow, ncol, nrep = sizes
    nh = nrep // 2
    group = ncol * nrep
    every = nrow * group
    slots = bbuf.shape[0]
    nodes, width = act_out.shape
    fw, col_nodes = igrad_out.shape
    pieces, cw = fbuf.shape[1], fbuf.shape[3]
    row_blocks, col_blocks = dense.shape[0] // 128, dense.shape[1] // 128
    r, c, p = lax.axis_index("row"), lax.axis_index("col"), lax.axis_index("rep")
    h, k = p // 2, p % 2
    g = c * nrep + p
    me = r * group + g
    partner = h * 2 + (1 - k)
    offsets = [(dc, dh) for dc in reversed(range(ncol)) for dh in reversed(range(nh))]
    chips = len(offsets)
    far = chips - 1
    last = nrow - 1
    at_end = (r == 0) | (r == last)

    def to_row(j):
        return {"row": (r + j) % nrow}

    def to_group(j):
        q = (g + j) % group
        return {"col": q // nrep, "rep": q % nrep}

    def to_any(j):
        q = (me + j) % every
        return {"row": q // group, "col": q % group // nrep, "rep": q % nrep}

    def to_chip(i):
        dc, dh = offsets[i]
        return {"col": (c + dc) % ncol, "rep": ((h + dh) % nh) * 2 + k}

    def part_to(i, core):
        dc, dh = offsets[i]
        return ((c + dc) % ncol) * nrep + ((h + dh) % nh) * 2 + core

    def part_from(i, core):
        dc, dh = offsets[i]
        return ((c + ncol - dc) % ncol) * nrep + ((h + nh - dh) % nh) * 2 + core

    def by_row(choices):
        value = choices[0]
        for q in range(1, nrow):
            value = jnp.where(r == q, choices[q], value)
        return value

    def nearest(n):
        return by_row([sorted(range(nrow), key=lambda t: (abs(t - q), t))[n] for q in range(nrow)])

    def turns(q):
        if q in (0, last):
            return sorted(range(nrow), key=lambda t: -abs(t - q))
        late = {1: last, last - 1: 0}.get(q)
        rest = [t for t in range(nrow) if t not in (q, late)]
        rest.sort(key=lambda t: (abs(t - q), abs(2 * t - last)))
        return rest + ([] if late is None else [late]) + [q]

    def turn(n):
        return by_row([turns(q)[n] for q in range(nrow)])

    def rcopy(src, dst, sems, n, device):
        return pltpu.make_async_remote_copy(
            src_ref=src,
            dst_ref=dst,
            send_sem=sems.at[0],
            recv_sem=sems.at[n + 1],
            device_id=device,
            device_id_type=MESH,
        )

    def await_all(ref, sem):
        pltpu.make_async_copy(ref, ref, sem).wait()

    barrier = pltpu.get_barrier_semaphore()
    for j in range(1, nrow):
        pl.semaphore_signal(barrier, inc=1, device_id=to_row(j), device_id_type=MESH)
    for j in range(1, group):
        pl.semaphore_signal(barrier, inc=1, device_id=to_group(j), device_id_type=MESH)

    def span(j):
        return slice(j * cw, (j + 1) * cw)

    feats = [
        pltpu.make_async_copy(feat_hbm.at[:, span(j)], fbuf.at[r, j], in_sem.at[0]) for j in range(pieces)
    ]
    others = [
        pltpu.make_async_copy(src, dst, in_sem.at[n + 1])
        for n, (src, dst) in enumerate(
            [
                (coords_hbm, coords_in),
                (count_hbm, count_in),
                (weight_hbm, weight_in),
                (cot_hbm, cot_in),
            ]
        )
    ]
    for copy in feats + others[:2]:
        copy.start()
    chunks = load_sem.shape[0]
    per = slots // chunks
    loads = []
    for i in range(chunks):
        there = pl.ds(i * per, per)
        loads.append(pltpu.make_async_copy(blocks_hbm.at[there], bbuf.at[there], load_sem.at[i]))
        loads[-1].start()
    for copy in others[2:]:
        copy.start()
    pl.semaphore_wait(barrier, nrow - 1 + group - 1)

    def feat_copy(src, slot, j, step):
        target = {"row": (r + nrow + step) % nrow}
        return rcopy(src, fbuf.at[slot, j], f_sem, slot * pieces + j, target)

    for j in range(pieces):
        for step, there in ((1, r < last), (-1, r > 0)):
            pl.when(there)(feat_copy(feat_hbm.at[:, span(j)], r, j, step).start)

    def relay(d, j):
        for slot, step, there in (
            (jnp.maximum(r - d, 0), 1, (r >= d) & (r < last)),
            (jnp.minimum(r + d, last), -1, (r + d <= last) & (r > 0)),
        ):

            @pl.when(there)
            def _(slot=slot, step=step):
                copy = feat_copy(fbuf.at[slot, j], slot, j, step)
                copy.wait_recv()
                copy.start()

    for copy in others[:2]:
        copy.wait()
    await_all(fbuf.at[r], in_sem.at[0])
    places = row_blocks * col_blocks
    live = count_in[0, 0]
    row_form = coords_in[0:1, :] * col_blocks + coords_in[1:2, :]
    column_form = jnp.broadcast_to(row_form, (slots, slots)).T
    mine_at = lax.broadcasted_iota(jnp.int32, (slots, slots), 0)
    other_at = lax.broadcasted_iota(jnp.int32, (slots, slots), 1)
    hit = (column_form == row_form) & (mine_at < jnp.minimum(other_at, live))
    tvec[0:1, 0:slots] = jnp.max(jnp.where(hit, mine_at + 1, 0), axis=0, keepdims=True)
    for start in range(0, places, slots):
        hit = (column_form == other_at + start) & (mine_at < live)
        tvec[0:1, slots + start : 2 * slots + start] = jnp.max(
            jnp.where(hit, mine_at + 1, 0), axis=0, keepdims=True
        )
    tcopy = pltpu.make_async_copy(tvec, table, t_sem)
    tcopy.start()
    tcopy.wait()

    sums[0] = jnp.zeros((128, 128), F32)
    for i in range(chunks):
        loads[i].wait()

        def add_slot(s, carry):
            sums[s + 1] = sums[table[0, s]] + bbuf[s].astype(F32)
            return carry

        lax.fori_loop(i * per, (i + 1) * per, add_slot, 0)

    def fill(rb, carry):
        for cb in range(col_blocks):
            block = sums[table[0, slots + rb * col_blocks + cb]]
            dense[pl.ds(rb * 128, 128), cb * 128 : (cb + 1) * 128] = block.astype(BF16)
        return carry

    lax.fori_loop(0, row_blocks, fill, 0)

    def partials(n, core):
        slot = nearest(n)
        rows = jnp.concatenate([fbuf[slot, j] for j in range(pieces)], axis=1)
        parts = [part_to(i, core) for i in range(chips)]
        return [dot(rows, dense[pl.ds(part * nodes, nodes), :], 1, 1) for part in parts]

    def merge(n):
        pcopies[n].wait_recv()
        for i in range(chips):
            both = ownp[n, i] + prec[n, i].astype(F32)
            if i == far:
                held[n] = both
            else:
                qbuf[n, i] = both.astype(BF16)
                rcopy(qbuf.at[n, i], qrec.at[n, i], q_sem, n, to_chip(i)).start()

    def collect(n):
        await_all(qrec.at[n], q_sem.at[n + 1])
        got = held[n]
        for i in range(far):
            got = got + qrec[n, i].astype(F32)
        agg[nearest(n)] = got.astype(BF16)

    relays = [(d, j) for d in range(1, nrow - 1) for j in range(pieces)]
    when = [min(n if n < 3 else n - 1, 2 * nrow - 2) for n in range(len(relays))]
    pcopies = []
    for n in range(nrow):
        for half in range(2):
            for at, (d, j) in zip(when, relays):
                if at == 2 * n + half:
                    relay(d, j)
            if half == 0:
                if n > 0:
                    slot = nearest(n)
                    for j in range(pieces):
                        copy = feat_copy(fbuf.at[slot, j], slot, j, 0)
                        pl.when(at_end)(copy.wait_recv)
                for i, part in enumerate(partials(n, 1 - k)):
                    pbuf[n, i] = part.astype(BF16)
                pcopies.append(rcopy(pbuf.at[n], prec.at[n], p_sem, n, {"rep": partner}))
                pcopies[n].start()
            else:
                for i, part in enumerate(partials(n, k)):
                    ownp[n, i] = part
                merge(n)
                if n > 1:
                    collect(n - 2)

    for copy in others[2:]:
        copy.wait()
    collect(last - 1)
    collect(last)

    aggregate = agg[...].reshape(width, nodes)
    pre_act = dot(aggregate, weight_in[...], 0, 0)
    sigma = jax.nn.sigmoid(pre_act)
    grad_pre = (cot_in[...].astype(F32) * sigma * (1.0 + pre_act * (1.0 - sigma))).astype(BF16)
    own_back[...] = dot(weight_in[...], grad_pre, 1, 1).astype(BF16).reshape(nrow, fw, nodes)

    def spread(n):
        for i in range(far):
            rcopy(own_back.at[turn(n)], brec.at[n, i], b_sem, n * far + i, to_chip(i)).start()

    ocopy = rcopy(own_back, bown, o_sem, 0, {"rep": partner})
    ocopy.start()
    spread(0)
    terms = dot(aggregate, grad_pre).astype(BF16)
    tr, tl = wbuf.shape[1:]
    wbuf[...] = jnp.concatenate(
        [terms[:, n * tl : (n + 1) * tl].reshape(width // tr, tr, tl) for n in range(width // tl)], axis=0
    )
    for j in range(1, every):
        rcopy(wbuf.at[(me + j) % every], wrec.at[j - 1], w_sem, 0, to_any(j)).start()
    for n in range(1, nrow):
        spread(n)
    act_out[...] = (pre_act * sigma).astype(BF16)
    results = [
        pltpu.make_async_copy(src, dst, in_sem.at[5 + n])
        for n, (src, dst) in enumerate(
            [(act_out, act_hbm), (igrad_out, igrad_hbm), (wgrad_out, wgrad_hbm)]
        )
    ]
    results[0].start()

    def back_term(piece_t, part):
        return dot(piece_t, dense[pl.ds(part * nodes, nodes), :])

    def begin(n):
        total[n] = back_term(own_back[turn(n)], g) + back_term(bown[turn(n)], c * nrep + partner)

    def middle(n):
        for i in reversed(range(far)):
            copy = rcopy(brec.at[n, i], bpar.at[n, i], c_sem, n, {"rep": partner})
            await_all(brec.at[n, i], b_sem.at[n * far + i + 1])
            copy.start()
            total[n] += back_term(brec[n, i], part_from(i, k))

    def finish(n):
        await_all(bpar.at[n], c_sem.at[n + 1])
        for i in reversed(range(far)):
            total[n] += back_term(bpar[n, i], part_from(i, 1 - k))

    halves = zbuf.shape[1]
    fh = fw // halves

    def zpart(n, m):
        return total[n, m * fh : (m + 1) * fh]

    def zcopy(n, m):
        q = turn(n)
        far_off = jnp.abs(q - r) == last
        inner = jnp.where(r == 0, 1, last - 1)
        lane = jnp.where(far_off, nrow, r)
        target = {"row": jnp.where(far_off, inner, q)}
        return rcopy(zbuf.at[n, m], zrec.at[lane, m], z_sem, lane + jnp.where(far_off, m, 0), target)

    joins = (r == 1) | (r == last - 1)
    ocopy.wait_recv()
    begin(0)
    for n in range(nrow):
        middle(n)
        if n < last:
            begin(n + 1)
        finish(n)
        if n < last:
            for m in range(halves):
                there = None if n < last - 1 else jnp.logical_not(joins)

                def put(n=n, m=m):
                    zbuf[n, m] = zpart(n, m).astype(BF16)
                    zcopy(n, m).start()

                if there is None:
                    put()
                else:
                    pl.when(there)(put)
        if n == 0:
            await_all(wrec, w_sem.at[1])
            share = wbuf[me].astype(F32)
            for j in range(every - 1):
                share = share + wrec[j].astype(F32)
            wrow[r] = share.astype(BF16)
            for j in range(1, nrow):
                rcopy(wrow.at[r], wrow.at[r], s_sem, 0, to_row(j)).start()

    for m in range(halves):

        @pl.when(joins)
        def _(m=m):
            await_all(zrec.at[nrow, m], z_sem.at[nrow + m + 1])
            zbuf[last - 1, m] = (zpart(last - 1, m) + zrec[nrow, m].astype(F32)).astype(BF16)
            zcopy(last - 1, m).start()

    await_all(wrow.at[pl.ds(0, last)], s_sem.at[1])
    wall[g] = wrow[...]
    for j in range(1, group):
        rcopy(wrow, wall.at[g], g_sem, 0, to_group(j)).start()

    for j in range(1, nrow):
        q = (r + j) % nrow

        @pl.when(jnp.abs(q - r) < last)
        def _(q=q):
            await_all(zrec.at[q], z_sem.at[q + 1])
            for m in range(halves):
                total[last, m * fh : (m + 1) * fh] += zrec[q, m].astype(F32)

    igrad_out[...] = total[last].astype(BF16)
    results[1].start()
    await_all(wall.at[pl.ds(0, group - 1)], g_sem.at[1])
    per_lane = width // tr
    for row in range(nrow):
        for q in range(group):
            n = row * group + q
            at, lane = n % per_lane * tr, n // per_lane * tl
            wgrad_out[at : at + tr, lane : lane + tl] = wall[q, row].astype(F32)
    results[2].start()
    pl.when(at_end)(lambda: await_all(fbuf.at[0], f_sem.at[0]))
    pl.when(jnp.logical_not(at_end))(lambda: await_all(zrec, f_sem.at[0]))
    await_all(pbuf, p_sem.at[0])
    await_all(qbuf, q_sem.at[0])
    await_all(brec, b_sem.at[0])
    await_all(own_back, o_sem.at[0])
    await_all(bpar, c_sem.at[0])
    await_all(zbuf, z_sem.at[0])
    await_all(wrec, w_sem.at[0])
    await_all(wrow.at[pl.ds(0, last)], s_sem.at[0])
    await_all(wall.at[pl.ds(0, group - 1)], g_sem.at[0])
    for copy in results:
        copy.wait()


def keep_kernel(a_in, b_in, c_in, a_out, b_out, c_out, sem):
    copies = [
        pltpu.make_async_copy(src, dst, sem.at[n])
        for n, (src, dst) in enumerate([(c_in, c_out), (a_in, a_out), (b_in, b_out)])
    ]
    for copy in copies:
        copy.start()
    for copy in copies:
        copy.wait()


def local_kernel(sizes, features, weight, cotangent, block_values, block_coords, block_counts):
    nrow, ncol, nrep = sizes
    group = ncol * nrep
    every = nrow * group
    chips = group // 2
    blocks = block_values[0, 0]
    slots = blocks.shape[0]
    nodes, width = cotangent.shape
    col_nodes, fw = features.shape
    row_blocks = nodes * group // 128
    places = row_blocks * (col_nodes // 128)
    chunks = math.gcd(slots, 4)
    pieces = math.gcd(col_nodes // 128, 4)
    vmem = functools.partial(pl.BlockSpec, memory_space=pltpu.VMEM)
    hbm = functools.partial(pl.BlockSpec, memory_space=pl.ANY)
    dma = pltpu.SemaphoreType.DMA
    block = (fw, nodes)
    tile = (width * width // every // 128, 128)
    outs = pl.pallas_call(
        functools.partial(layer_kernel, sizes),
        out_shape=(
            pltpu.VMEM((nodes, width), BF16),
            pltpu.VMEM((fw, col_nodes), BF16),
            pltpu.VMEM((width, width), F32),
        ),
        in_specs=[hbm()] * 6,
        out_specs=(hbm(), hbm(), hbm()),
        scratch_shapes=[
            pltpu.VMEM((nodes, width), BF16),
            pltpu.VMEM((fw, col_nodes), BF16),
            pltpu.VMEM((width, width), F32),
            pltpu.SMEM((1, 1), jnp.int32),
            pltpu.VMEM((2, slots), jnp.int32),
            pltpu.VMEM((width, width), BF16),
            pltpu.VMEM((nodes, width), BF16),
            pltpu.VMEM((nrow, pieces, fw, col_nodes // pieces), BF16),
            pltpu.VMEM((slots, 128, 128), BF16),
            pltpu.VMEM((slots + 1, 128, 128), F32),
            pltpu.VMEM((row_blocks * 128, col_nodes), BF16),
            pltpu.VMEM((nrow, chips) + block, BF16),
            pltpu.VMEM((nrow, chips) + block, BF16),
            pltpu.VMEM((nrow, chips) + block, F32),
            pltpu.VMEM((nrow, chips - 1) + block, BF16),
            pltpu.VMEM((nrow, chips - 1) + block, BF16),
            pltpu.VMEM((nrow,) + block, F32),
            pltpu.VMEM((nrow,) + block, BF16),
            pltpu.VMEM((nrow,) + block, BF16),
            pltpu.VMEM((nrow,) + block, BF16),
            pltpu.VMEM((nrow, chips - 1) + block, BF16),
            pltpu.VMEM((nrow, chips - 1) + block, BF16),
            pltpu.VMEM((nrow, fw, col_nodes), F32),
            pltpu.VMEM((nrow - 1, 2, fw // 2, col_nodes), BF16),
            pltpu.VMEM((nrow + 1, 2, fw // 2, col_nodes), BF16),
            pltpu.VMEM((every,) + tile, BF16),
            pltpu.VMEM((every - 1,) + tile, BF16),
            pltpu.VMEM((nrow,) + tile, BF16),
            pltpu.VMEM((group, nrow) + tile, BF16),
            pltpu.VMEM((1, slots + places), jnp.int32),
            pltpu.SMEM((1, slots + places), jnp.int32),
            dma((chunks,)),
            dma((8,)),
            dma,
            dma((1 + nrow * pieces,)),
            dma((1 + nrow,)),
            dma((1 + nrow,)),
            dma((1 + nrow * (chips - 1),)),
            dma((2,)),
            dma((1 + nrow,)),
            dma((3 + nrow,)),
            dma((2,)),
            dma((2,)),
            dma((2,)),
        ],
        compiler_params=pltpu.CompilerParams(
            collective_id=0, has_side_effects=True, vmem_limit_bytes=VMEM_BUDGET
        ),
    )(block_counts, block_coords[0, 0].T, features.T, weight, cotangent, blocks)
    activations, input_grad_t, weight_grad = pl.pallas_call(
        keep_kernel,
        out_shape=tuple(jax.ShapeDtypeStruct(x.shape, x.dtype) for x in outs),
        in_specs=[hbm()] * 3,
        out_specs=(hbm(),) * 3,
        scratch_shapes=[dma((3,))],
    )(*[pltpu.with_memory_space_constraint(x, pltpu.VMEM) for x in outs])
    return activations, input_grad_t.T, weight_grad


def fits(mesh, features, weight, cotangent, block_values):
    nrow, ncol, nrep = (mesh.shape[name] for name in ("row", "col", "rep"))
    group = ncol * nrep
    width = features.shape[1]
    fw = width // nrow
    rows, cols = cotangent.shape[0] // nrow, features.shape[0] // group
    tile = rows * cols * 2 + block_values.shape[2] * 128 * 128 * 6
    moved = 8 * rows * width + 12 * cols * width
    whole = nrep % 2 == 0 and block_values.shape[2] == 128 and rows * cols % 128**3 == 0
    whole = whole and fw % 32 == 0 and width % 128 == 0 and width**2 % (2048 * nrow * group) == 0
    return whole and nrow > 3 and group > 2 and tile + moved < VMEM_BUDGET * 3 // 4


def solution(mesh):
    in_specs = (
        P(("col", "rep"), "row"),
        P(),
        P(("row", "col", "rep"), None),
        P("row", ("col", "rep"), None, None, None),
        P("row", ("col", "rep"), None, None),
        P("row", ("col", "rep")),
    )
    out_specs = (P(("row", "col", "rep"), None), P(("col", "rep"), "row"), P())
    sizes = tuple(mesh.shape[name] for name in ("row", "col", "rep"))

    def run(features, weight, cotangent, block_values, block_coords, block_counts):
        if fits(mesh, features, weight, cotangent, block_values):
            body = functools.partial(local_kernel, sizes)
        else:
            body = local_xla
        return jax.shard_map(
            body, mesh=mesh, in_specs=in_specs, out_specs=out_specs, check_vma=False
        )(features, weight, cotangent, block_values, block_coords, block_counts)

    return run
```

time: 51.3 us -> 44.3 us (0.86)
  Pallas kernels: 49.9 us -> 42.8 us
    pallas_call x1, Pallas kernels: 48 us -> 42 us  [local_kernel(): pl.pallas_call(functools.partial(layer_kernel, sizes), out_shape=(pltpu.V...]
    pallas_call x1, Pallas kernels: 1.88 us -> 0.81 us  [local_kernel(): pl.pallas_call(keep_kernel, out_shape=tuple((jax.ShapeDtypeStruct(x.shape...]
where the time goes in v1:
time: 44.3 us; the launch traced here: 44.1 us
  Pallas kernels  42.8 us (97%)
  between operations  1.29 us (3%)
    pallas_call x1, Pallas kernels, local_kernel(): pl.pallas_call(functools.partial(layer_kernel, sizes), out_shape=(pltpu.V...  42 us

profile of v1, /device:TPU:0, one launch (start us, length us, event | category | flops | bytes accessed | tf_op | source)
XLA Modules:
  0.0 44.1 jit_solution(151463399702363476)
XLA Ops:
  1.3 42.0 %shard_map.85 = (bf16[256,256]{1,0:T(8,128)(2,1)S(1)}, bf16[64,1024]{1,0:T(8,128)(2,1)S(1)}, f32[256,256]{1,0:T(8,128)S(1)}) custom-call(s32[1,1]{1,0:T(1,128)S(6)} %copy.9.count_hbm, s32[2,128]{1,0:T(2,128)} %bitcast.8, bf16[64,1024]{1,0:T(8,128)(2,1)} %bitcast.7, bf16[256,256]{1,0:T(8,128)(2,1)} %weight_hbm.1, bf16[256,256]{1,0:T(8,128)(2,1)} %cot_hbm.1, ...), custom_call_target="tpu_custom_call" | custom-call | tf_op jit(solution)/shard_map/pallas_call | solution.py:533
  43.3 0.8 %shard_map.86 = (bf16[256,256]{1,0:T(8,128)(2,1)}, bf16[64,1024]{1,0:T(8,128)(2,1)}, f32[256,256]{1,0:T(8,128)}) custom-call(bf16[256,256]{1,0:T(8,128)(2,1)S(1)} %get-tuple-element.9.a_in, bf16[64,1024]{1,0:T(8,128)(2,1)S(1)} %get-tuple-element.10.b_in, f32[256,256]{1,0:T(8,128)S(1)} %get-tuple-element.11.c_in), custom_call_target="tpu_custom_call" | custom-call | tf_op jit(solution)/shard_map/pallas_call | solution.py:592

commit v2 on v1

--- a/solution.py
+++ b/solution.py
@@ -108,6 +108,8 @@
     pbuf,
     prec,
     ownp,
+    accp,
+    acco,
     qbuf,
     qrec,
     held,
@@ -158,6 +160,7 @@
     far = chips - 1
     last = nrow - 1
     at_end = (r == 0) | (r == last)
+    joints = [(1, last, last - 1), (last - 1, 0, 1)]
 
     def to_row(j):
         return {"row": (r + j) % nrow}
@@ -192,12 +195,17 @@
         return by_row([sorted(range(nrow), key=lambda t: (abs(t - q), t))[n] for q in range(nrow)])
 
     def turns(q):
-        if q in (0, last):
-            return sorted(range(nrow), key=lambda t: -abs(t - q))
-        late = {1: last, last - 1: 0}.get(q)
-        rest = [t for t in range(nrow) if t not in (q, late)]
+        rest = [t for t in range(nrow) if t != q]
+        if q == 0:
+            return rest[::-1] + [q]
+        if q == last:
+            return [0] + rest[:0:-1] + [q]
         rest.sort(key=lambda t: (abs(t - q), abs(2 * t - last)))
-        return rest + ([] if late is None else [late]) + [q]
+        for row, passed, n in joints:
+            if row == q:
+                rest.remove(passed)
+                rest.insert(n, passed)
+        return rest + [q]
 
     def turn(n):
         return by_row([turns(q)[n] for q in range(nrow)])
@@ -214,12 +222,6 @@
 
     def await_all(ref, sem):
         pltpu.make_async_copy(ref, ref, sem).wait()
-
-    barrier = pltpu.get_barrier_semaphore()
-    for j in range(1, nrow):
-        pl.semaphore_signal(barrier, inc=1, device_id=to_row(j), device_id_type=MESH)
-    for j in range(1, group):
-        pl.semaphore_signal(barrier, inc=1, device_id=to_group(j), device_id_type=MESH)
 
     def span(j):
         return slice(j * cw, (j + 1) * cw)
@@ -238,7 +240,15 @@
             ]
         )
     ]
-    for copy in feats + others[:2]:
+    for copy in feats:
+        copy.start()
+
+    barrier = pltpu.get_barrier_semaphore()
+    for j in range(1, nrow):
+        pl.semaphore_signal(barrier, inc=1, device_id=to_row(j), device_id_type=MESH)
+    for j in range(1, group):
+        pl.semaphore_signal(barrier, inc=1, device_id=to_group(j), device_id_type=MESH)
+    for copy in others[:2]:
         copy.start()
     chunks = load_sem.shape[0]
     per = slots // chunks
@@ -249,6 +259,7 @@
         loads[-1].start()
     for copy in others[2:]:
         copy.start()
+    await_all(fbuf.at[r], in_sem.at[0])
     pl.semaphore_wait(barrier, nrow - 1 + group - 1)
 
     def feat_copy(src, slot, j, step):
@@ -257,7 +268,7 @@
 
     for j in range(pieces):
         for step, there in ((1, r < last), (-1, r > 0)):
-            pl.when(there)(feat_copy(feat_hbm.at[:, span(j)], r, j, step).start)
+            pl.when(there)(feat_copy(fbuf.at[r, j], r, j, step).start)
 
     def relay(d, j):
         for slot, step, there in (
@@ -273,7 +284,6 @@
 
     for copy in others[:2]:
         copy.wait()
-    await_all(fbuf.at[r], in_sem.at[0])
     places = row_blocks * col_blocks
     live = count_in[0, 0]
     row_form = coords_in[0:1, :] * col_blocks + coords_in[1:2, :]
@@ -309,11 +319,15 @@
 
     lax.fori_loop(0, row_blocks, fill, 0)
 
-    def partials(n, core):
-        slot = nearest(n)
-        rows = jnp.concatenate([fbuf[slot, j] for j in range(pieces)], axis=1)
+    def partials(n, core, reach):
+        slot, (low, high) = nearest(n), reach
+        rows = jnp.concatenate([fbuf[slot, j] for j in range(low, high)], axis=1)
         parts = [part_to(i, core) for i in range(chips)]
-        return [dot(rows, dense[pl.ds(part * nodes, nodes), :], 1, 1) for part in parts]
+        cols = slice(low * cw, high * cw)
+        return [dot(rows, dense[pl.ds(part * nodes, nodes), cols], 1, 1) for part in parts]
+
+    def tail(n):
+        return (0 if n < last else pieces - 1, pieces)
 
     def merge(n):
         pcopies[n].wait_recv()
@@ -333,7 +347,7 @@
         agg[nearest(n)] = got.astype(BF16)
 
     relays = [(d, j) for d in range(1, nrow - 1) for j in range(pieces)]
-    when = [min(n if n < 3 else n - 1, 2 * nrow - 2) for n in range(len(relays))]
+    when = [min((0, 1, 2, 2, 3, 4, 4, 5)[n % 8] + n // 8 * 4, 2 * nrow - 2) for n in range(len(relays))]
     pcopies = []
     for n in range(nrow):
         for half in range(2):
@@ -346,13 +360,17 @@
                     for j in range(pieces):
                         copy = feat_copy(fbuf.at[slot, j], slot, j, 0)
                         pl.when(at_end)(copy.wait_recv)
-                for i, part in enumerate(partials(n, 1 - k)):
-                    pbuf[n, i] = part.astype(BF16)
+                        if n == last and 0 < j < pieces - 1:
+                            for core, sofar in ((1 - k, accp), (k, acco)):
+                                for i, part in enumerate(partials(n, core, (0 if j == 1 else j, j + 1))):
+                                    sofar[i] = part if j == 1 else sofar[i] + part
+                for i, part in enumerate(partials(n, 1 - k, tail(n))):
+                    pbuf[n, i] = (part if n < last else accp[i] + part).astype(BF16)
                 pcopies.append(rcopy(pbuf.at[n], prec.at[n], p_sem, n, {"rep": partner}))
                 pcopies[n].start()
             else:
-                for i, part in enumerate(partials(n, k)):
-                    ownp[n, i] = part
+                for i, part in enumerate(partials(n, k, tail(n))):
+                    ownp[n, i] = part if n < last else acco[i] + part
                 merge(n)
                 if n > 1:
                     collect(n - 2)
@@ -368,13 +386,19 @@
     grad_pre = (cot_in[...].astype(F32) * sigma * (1.0 + pre_act * (1.0 - sigma))).astype(BF16)
     own_back[...] = dot(weight_in[...], grad_pre, 1, 1).astype(BF16).reshape(nrow, fw, nodes)
 
-    def spread(n):
+    units = [(0, m, fw // 2) for m in (0, fw // 2)] + [(n, 0, fw) for n in range(1, nrow)]
+
+    def spread(u):
+        n, at, size = units[u]
+        rows = pl.ds(at, size)
         for i in range(far):
-            rcopy(own_back.at[turn(n)], brec.at[n, i], b_sem, n * far + i, to_chip(i)).start()
+            src, dst = own_back.at[turn(n), rows], brec.at[n, i, rows]
+            rcopy(src, dst, b_sem, u * far + i, to_chip(i)).start()
 
     ocopy = rcopy(own_back, bown, o_sem, 0, {"rep": partner})
+    spread(0)
     ocopy.start()
-    spread(0)
+    spread(1)
     terms = dot(aggregate, grad_pre).astype(BF16)
     tr, tl = wbuf.shape[1:]
     wbuf[...] = jnp.concatenate(
@@ -382,8 +406,8 @@
     )
     for j in range(1, every):
         rcopy(wbuf.at[(me + j) % every], wrec.at[j - 1], w_sem, 0, to_any(j)).start()
-    for n in range(1, nrow):
-        spread(n)
+    for u in range(2, len(units)):
+        spread(u)
     act_out[...] = (pre_act * sigma).astype(BF16)
     results = [
         pltpu.make_async_copy(src, dst, in_sem.at[5 + n])
@@ -399,20 +423,24 @@
     def begin(n):
         total[n] = back_term(own_back[turn(n)], g) + back_term(bown[turn(n)], c * nrep + partner)
 
-    def middle(n):
+    def middle(u):
+        n, at, size = units[u]
+        rows = pl.ds(at, size)
         for i in reversed(range(far)):
-            copy = rcopy(brec.at[n, i], bpar.at[n, i], c_sem, n, {"rep": partner})
-            await_all(brec.at[n, i], b_sem.at[n * far + i + 1])
+            copy = rcopy(brec.at[n, i, rows], bpar.at[n, i, rows], c_sem, u, {"rep": partner})
+            await_all(brec.at[n, i, rows], b_sem.at[u * far + i + 1])
             copy.start()
-            total[n] += back_term(brec[n, i], part_from(i, k))
-
-    def finish(n):
-        await_all(bpar.at[n], c_sem.at[n + 1])
+            total[n, rows] += back_term(brec[n, i, rows], part_from(i, k))
+
+    def finish(u):
+        n, at, size = units[u]
+        rows = pl.ds(at, size)
+        await_all(bpar.at[n, :, rows], c_sem.at[u + 1])
         for i in reversed(range(far)):
-            total[n] += back_term(bpar[n, i], part_from(i, 1 - k))
-
-    halves = zbuf.shape[1]
-    fh = fw // halves
+            total[n, rows] += back_term(bpar[n, i, rows], part_from(i, 1 - k))
+
+    steps = zbuf.shape[1]
+    fh = fw // steps
 
     def zpart(n, m):
         return total[n, m * fh : (m + 1) * fh]
@@ -425,27 +453,39 @@
         target = {"row": jnp.where(far_off, inner, q)}
         return rcopy(zbuf.at[n, m], zrec.at[lane, m], z_sem, lane + jnp.where(far_off, m, 0), target)
 
-    joins = (r == 1) | (r == last - 1)
     ocopy.wait_recv()
     begin(0)
-    for n in range(nrow):
-        middle(n)
+
+    def join(n, span):
+        for row, _, at in joints:
+            if at == n:
+
+                @pl.when(r == row)
+                def _():
+                    for m in span:
+                        await_all(zrec.at[nrow, m], z_sem.at[nrow + m + 1])
+                        zbuf[n, m] = (zpart(n, m) + zrec[nrow, m].astype(F32)).astype(BF16)
+                        zcopy(n, m).start()
+
+    for u, (n, at, size) in enumerate(units):
+        middle(u)
+        if u > 0 and n < last:
+            begin(n + 1)
+        if u > 0 and n > 0:
+            join(n - 1, range(steps // 2))
+        finish(u)
         if n < last:
-            begin(n + 1)
-        finish(n)
-        if n < last:
-            for m in range(halves):
-                there = None if n < last - 1 else jnp.logical_not(joins)
-
-                def put(n=n, m=m):
+
+            def put(n=n, at=at, size=size):
+                for m in range(at // fh, (at + size) // fh):
                     zbuf[n, m] = zpart(n, m).astype(BF16)
                     zcopy(n, m).start()
 
-                if there is None:
-                    put()
-                else:
-                    pl.when(there)(put)
-        if n == 0:
+            keep = functools.reduce(jnp.logical_and, [r != row for row, _, at in joints if at == n], r >= 0)
+            pl.when(keep)(put)
+        if n > 0:
+            join(n - 1, range(steps // 2, steps))
+        if u == 1:
             await_all(wrec, w_sem.at[1])
             share = wbuf[me].astype(F32)
             for j in range(every - 1):
@@ -454,14 +494,6 @@
             for j in range(1, nrow):
                 rcopy(wrow.at[r], wrow.at[r], s_sem, 0, to_row(j)).start()
 
-    for m in range(halves):
-
-        @pl.when(joins)
-        def _(m=m):
-            await_all(zrec.at[nrow, m], z_sem.at[nrow + m + 1])
-            zbuf[last - 1, m] = (zpart(last - 1, m) + zrec[nrow, m].astype(F32)).astype(BF16)
-            zcopy(last - 1, m).start()
-
     await_all(wrow.at[pl.ds(0, last)], s_sem.at[1])
     wall[g] = wrow[...]
     for j in range(1, group):
@@ -473,7 +505,7 @@
         @pl.when(jnp.abs(q - r) < last)
         def _(q=q):
             await_all(zrec.at[q], z_sem.at[q + 1])
-            for m in range(halves):
+            for m in range(steps):
                 total[last, m * fh : (m + 1) * fh] += zrec[q, m].astype(F32)
 
     igrad_out[...] = total[last].astype(BF16)
@@ -537,7 +569,7 @@
             pltpu.VMEM((fw, col_nodes), BF16),
             pltpu.VMEM((width, width), F32),
         ),
-        in_specs=[hbm()] * 6,
+        in_specs=[pl.BlockSpec(memory_space=pltpu.HBM)] + [hbm()] * 5,
         out_specs=(hbm(), hbm(), hbm()),
         scratch_shapes=[
             pltpu.VMEM((nodes, width), BF16),
@@ -554,6 +586,8 @@
             pltpu.VMEM((nrow, chips) + block, BF16),
             pltpu.VMEM((nrow, chips) + block, BF16),
             pltpu.VMEM((nrow, chips) + block, F32),
+            pltpu.VMEM((chips,) + block, F32),
+            pltpu.VMEM((chips,) + block, F32),
             pltpu.VMEM((nrow, chips - 1) + block, BF16),
             pltpu.VMEM((nrow, chips - 1) + block, BF16),
             pltpu.VMEM((nrow,) + block, F32),
@@ -563,8 +597,8 @@
             pltpu.VMEM((nrow, chips - 1) + block, BF16),
             pltpu.VMEM((nrow, chips - 1) + block, BF16),
             pltpu.VMEM((nrow, fw, col_nodes), F32),
-            pltpu.VMEM((nrow - 1, 2, fw // 2, col_nodes), BF16),
-            pltpu.VMEM((nrow + 1, 2, fw // 2, col_nodes), BF16),
+            pltpu.VMEM((nrow - 1, 4, fw // 4, col_nodes), BF16),
+            pltpu.VMEM((nrow + 1, 4, fw // 4, col_nodes), BF16),
             pltpu.VMEM((every,) + tile, BF16),
             pltpu.VMEM((every - 1,) + tile, BF16),
             pltpu.VMEM((nrow,) + tile, BF16),
@@ -577,10 +611,10 @@
             dma((1 + nrow * pieces,)),
             dma((1 + nrow,)),
             dma((1 + nrow,)),
-            dma((1 + nrow * (chips - 1),)),
+            dma((1 + (nrow + 1) * (chips - 1),)),
             dma((2,)),
-            dma((1 + nrow,)),
-            dma((3 + nrow,)),
+            dma((2 + nrow,)),
+            dma((5 + nrow,)),
             dma((2,)),
             dma((2,)),
             dma((2,)),
@@ -608,7 +642,7 @@
     tile = rows * cols * 2 + block_values.shape[2] * 128 * 128 * 6
     moved = 8 * rows * width + 12 * cols * width
     whole = nrep % 2 == 0 and block_values.shape[2] == 128 and rows * cols % 128**3 == 0
-    whole = whole and fw % 32 == 0 and width % 128 == 0 and width**2 % (2048 * nrow * group) == 0
+    whole = whole and fw % 64 == 0 and width % 128 == 0 and width**2 % (2048 * nrow * group) == 0
     return whole and nrow > 3 and group > 2 and tile + moved < VMEM_BUDGET * 3 // 4
 
 

time: 44.3 us -> 41.3 us (0.932)
  Pallas kernels: 42.8 us -> 39.9 us
    pallas_call x1, Pallas kernels: 42 us -> 39 us  [local_kernel(): pl.pallas_call(functools.partial(layer_kernel, sizes), out_shape=(pltpu.V...]
where the time goes in v2:
time: 41.3 us; the launch traced here: 41.1 us
  Pallas kernels  39.9 us (97%)
  between operations  1.29 us (3%)
    pallas_call x1, Pallas kernels, local_kernel(): pl.pallas_call(functools.partial(layer_kernel, sizes), out_shape=(pltpu.V...  39 us

profile of v2, /device:TPU:0, one launch (start us, length us, event | category | flops | bytes accessed | tf_op | source)
XLA Modules:
  0.0 41.1 jit_solution(12187662057884690026)
XLA Ops:
  1.3 39.0 %shard_map.85 = (bf16[256,256]{1,0:T(8,128)(2,1)S(1)}, bf16[64,1024]{1,0:T(8,128)(2,1)S(1)}, f32[256,256]{1,0:T(8,128)S(1)}) custom-call(s32[1,1]{1,0:T(1,128)S(6)} %copy.9.count_hbm, s32[2,128]{1,0:T(2,128)} %bitcast.8, bf16[64,1024]{1,0:T(8,128)(2,1)} %bitcast.7, bf16[256,256]{1,0:T(8,128)(2,1)} %weight_hbm.1, bf16[256,256]{1,0:T(8,128)(2,1)} %cot_hbm.1, ...), custom_call_target="tpu_custom_call" | custom-call | tf_op jit(solution)/shard_map/pallas_call | solution.py:565
  40.3 0.8 %shard_map.86 = (bf16[256,256]{1,0:T(8,128)(2,1)}, bf16[64,1024]{1,0:T(8,128)(2,1)}, f32[256,256]{1,0:T(8,128)}) custom-call(bf16[256,256]{1,0:T(8,128)(2,1)S(1)} %get-tuple-element.9.a_in, bf16[64,1024]{1,0:T(8,128)(2,1)S(1)} %get-tuple-element.10.b_in, f32[256,256]{1,0:T(8,128)S(1)} %get-tuple-element.11.c_in), custom_call_target="tpu_custom_call" | custom-call | tf_op jit(solution)/shard_map/pallas_call | solution.py:626

commit v3 on v2

--- a/solution.py
+++ b/solution.py
@@ -399,6 +399,7 @@
     spread(0)
     ocopy.start()
     spread(1)
+    spread(2)
     terms = dot(aggregate, grad_pre).astype(BF16)
     tr, tl = wbuf.shape[1:]
     wbuf[...] = jnp.concatenate(
@@ -406,7 +407,7 @@
     )
     for j in range(1, every):
         rcopy(wbuf.at[(me + j) % every], wrec.at[j - 1], w_sem, 0, to_any(j)).start()
-    for u in range(2, len(units)):
+    for u in range(3, len(units)):
         spread(u)
     act_out[...] = (pre_act * sigma).astype(BF16)
     results = [
@@ -467,25 +468,19 @@
                         zbuf[n, m] = (zpart(n, m) + zrec[nrow, m].astype(F32)).astype(BF16)
                         zcopy(n, m).start()
 
+    def advance(u):
+        if u < len(units):
+            if units[u][1] == 0 and u > 0:
+                begin(units[u][0])
+            middle(u)
+
+    middle(0)
     for u, (n, at, size) in enumerate(units):
-        middle(u)
-        if u > 0 and n < last:
-            begin(n + 1)
+        pl.when(k == 1)(lambda: advance(u + 1))
         if u > 0 and n > 0:
             join(n - 1, range(steps // 2))
         finish(u)
-        if n < last:
-
-            def put(n=n, at=at, size=size):
-                for m in range(at // fh, (at + size) // fh):
-                    zbuf[n, m] = zpart(n, m).astype(BF16)
-                    zcopy(n, m).start()
-
-            keep = functools.reduce(jnp.logical_and, [r != row for row, _, at in joints if at == n], r >= 0)
-            pl.when(keep)(put)
-        if n > 0:
-            join(n - 1, range(steps // 2, steps))
-        if u == 1:
+        if n == 1:
             await_all(wrec, w_sem.at[1])
             share = wbuf[me].astype(F32)
             for j in range(every - 1):
@@ -493,6 +488,18 @@
             wrow[r] = share.astype(BF16)
             for j in range(1, nrow):
                 rcopy(wrow.at[r], wrow.at[r], s_sem, 0, to_row(j)).start()
+        if n < last:
+
+            def put(n=n, at=at, size=size):
+                for m in range(at // fh, (at + size) // fh):
+                    zbuf[n, m] = zpart(n, m).astype(BF16)
+                    zcopy(n, m).start()
+
+            keep = functools.reduce(jnp.logical_and, [r != row for row, _, at in joints if at == n], r >= 0)
+            pl.when(keep)(put)
+        pl.when(k == 0)(lambda: advance(u + 1))
+        if n > 0:
+            join(n - 1, range(steps // 2, steps))
 
     await_all(wrow.at[pl.ds(0, last)], s_sem.at[1])
     wall[g] = wrow[...]

time: 41.3 us -> 40.4 us (0.978)
  Pallas kernels: 39.9 us -> 39 us
    pallas_call x1, Pallas kernels: 39 us -> 38.2 us  [local_kernel(): pl.pallas_call(functools.partial(layer_kernel, sizes), out_shape=(pltpu.V...]
where the time goes in v3:
time: 40.4 us; the launch traced here: 40.3 us
  Pallas kernels  39 us (97%)
  between operations  1.29 us (3%)
    pallas_call x1, Pallas kernels, local_kernel(): pl.pallas_call(functools.partial(layer_kernel, sizes), out_shape=(pltpu.V...  38.2 us
    pallas_call x1, Pallas kernels, local_kernel(): pl.pallas_call(keep_kernel, out_shape=tuple((jax.ShapeDtypeStruct(x.shape...  0.81 us

profile of v3, /device:TPU:0, one launch (start us, length us, event | category | flops | bytes accessed | tf_op | source)
XLA Modules:
  0.0 40.3 jit_solution(9758840432740855385)
XLA Ops:
  1.3 38.2 %shard_map.85 = (bf16[256,256]{1,0:T(8,128)(2,1)S(1)}, bf16[64,1024]{1,0:T(8,128)(2,1)S(1)}, f32[256,256]{1,0:T(8,128)S(1)}) custom-call(s32[1,1]{1,0:T(1,128)S(6)} %copy.9.count_hbm, s32[2,128]{1,0:T(2,128)} %bitcast.8, bf16[64,1024]{1,0:T(8,128)(2,1)} %bitcast.7, bf16[256,256]{1,0:T(8,128)(2,1)} %weight_hbm.1, bf16[256,256]{1,0:T(8,128)(2,1)} %cot_hbm.1, ...), custom_call_target="tpu_custom_call" | custom-call | tf_op jit(solution)/shard_map/pallas_call | solution.py:572
  39.4 0.8 %shard_map.86 = (bf16[256,256]{1,0:T(8,128)(2,1)}, bf16[64,1024]{1,0:T(8,128)(2,1)}, f32[256,256]{1,0:T(8,128)}) custom-call(bf16[256,256]{1,0:T(8,128)(2,1)S(1)} %get-tuple-element.9.a_in, bf16[64,1024]{1,0:T(8,128)(2,1)S(1)} %get-tuple-element.10.b_in, f32[256,256]{1,0:T(8,128)S(1)} %get-tuple-element.11.c_in), custom_call_target="tpu_custom_call" | custom-call | tf_op jit(solution)/shard_map/pallas_call | solution.py:633

commit v4 on v3

--- a/solution.py
+++ b/solution.py
@@ -133,7 +133,6 @@
     f_sem,
     p_sem,
     q_sem,
-    b_sem,
     o_sem,
     c_sem,
     z_sem,
@@ -377,6 +376,8 @@
 
     for copy in others[2:]:
         copy.wait()
+    pl.when(at_end)(lambda: await_all(fbuf.at[0], f_sem.at[0]))
+    pl.when(jnp.logical_not(at_end))(lambda: await_all(zrec, f_sem.at[0]))
     collect(last - 1)
     collect(last)
 
@@ -393,7 +394,7 @@
         rows = pl.ds(at, size)
         for i in range(far):
             src, dst = own_back.at[turn(n), rows], brec.at[n, i, rows]
-            rcopy(src, dst, b_sem, u * far + i, to_chip(i)).start()
+            rcopy(src, dst, f_sem, u * far + i, to_chip(i)).start()
 
     ocopy = rcopy(own_back, bown, o_sem, 0, {"rep": partner})
     spread(0)
@@ -411,7 +412,7 @@
         spread(u)
     act_out[...] = (pre_act * sigma).astype(BF16)
     results = [
-        pltpu.make_async_copy(src, dst, in_sem.at[5 + n])
+        pltpu.make_async_copy(src, dst, load_sem.at[n])
         for n, (src, dst) in enumerate(
             [(act_out, act_hbm), (igrad_out, igrad_hbm), (wgrad_out, wgrad_hbm)]
         )
@@ -429,7 +430,7 @@
         rows = pl.ds(at, size)
         for i in reversed(range(far)):
             copy = rcopy(brec.at[n, i, rows], bpar.at[n, i, rows], c_sem, u, {"rep": partner})
-            await_all(brec.at[n, i, rows], b_sem.at[u * far + i + 1])
+            await_all(brec.at[n, i, rows], f_sem.at[u * far + i + 1])
             copy.start()
             total[n, rows] += back_term(brec[n, i, rows], part_from(i, k))
 
@@ -525,11 +526,9 @@
             at, lane = n % per_lane * tr, n // per_lane * tl
             wgrad_out[at : at + tr, lane : lane + tl] = wall[q, row].astype(F32)
     results[2].start()
-    pl.when(at_end)(lambda: await_all(fbuf.at[0], f_sem.at[0]))
-    pl.when(jnp.logical_not(at_end))(lambda: await_all(zrec, f_sem.at[0]))
     await_all(pbuf, p_sem.at[0])
     await_all(qbuf, q_sem.at[0])
-    await_all(brec, b_sem.at[0])
+    await_all(brec, f_sem.at[0])
     await_all(own_back, o_sem.at[0])
     await_all(bpar, c_sem.at[0])
     await_all(zbuf, z_sem.at[0])
@@ -613,12 +612,11 @@
             pltpu.VMEM((1, slots + places), jnp.int32),
             pltpu.SMEM((1, slots + places), jnp.int32),
             dma((chunks,)),
-            dma((8,)),
+            dma((5,)),
             dma,
-            dma((1 + nrow * pieces,)),
+            dma((1 + max(nrow * pieces, (nrow + 1) * (chips - 1)),)),
             dma((1 + nrow,)),
             dma((1 + nrow,)),
-            dma((1 + (nrow + 1) * (chips - 1),)),
             dma((2,)),
             dma((2 + nrow,)),
             dma((5 + nrow,)),

time: 40.4 us -> 40.2 us (level)
  no operation moved by 1% of the time
where the time goes in v4:
time: 40.2 us; the launch traced here: 40.1 us
  Pallas kernels  38.8 us (97%)
  between operations  1.29 us (3%)
    pallas_call x1, Pallas kernels, local_kernel(): pl.pallas_call(functools.partial(layer_kernel, sizes), out_shape=(pltpu.V...  38 us
    pallas_call x1, Pallas kernels, local_kernel(): pl.pallas_call(keep_kernel, out_shape=tuple((jax.ShapeDtypeStruct(x.shape...  0.81 us

profile of v4, /device:TPU:0, one launch (start us, length us, event | category | flops | bytes accessed | tf_op | source)
XLA Modules:
  0.0 40.1 jit_solution(7538510164491055294)
XLA Ops:
  1.3 38.0 %shard_map.85 = (bf16[256,256]{1,0:T(8,128)(2,1)S(1)}, bf16[64,1024]{1,0:T(8,128)(2,1)S(1)}, f32[256,256]{1,0:T(8,128)S(1)}) custom-call(s32[1,1]{1,0:T(1,128)S(6)} %copy.9.count_hbm, s32[2,128]{1,0:T(2,128)} %bitcast.8, bf16[64,1024]{1,0:T(8,128)(2,1)} %bitcast.7, bf16[256,256]{1,0:T(8,128)(2,1)} %weight_hbm.1, bf16[256,256]{1,0:T(8,128)(2,1)} %cot_hbm.1, ...), custom_call_target="tpu_custom_call" | custom-call | tf_op jit(solution)/shard_map/pallas_call | solution.py:571
  39.3 0.8 %shard_map.86 = (bf16[256,256]{1,0:T(8,128)(2,1)}, bf16[64,1024]{1,0:T(8,128)(2,1)}, f32[256,256]{1,0:T(8,128)}) custom-call(bf16[256,256]{1,0:T(8,128)(2,1)S(1)} %get-tuple-element.9.a_in, bf16[64,1024]{1,0:T(8,128)(2,1)S(1)} %get-tuple-element.10.b_in, f32[256,256]{1,0:T(8,128)S(1)} %get-tuple-element.11.c_in), custom_call_target="tpu_custom_call" | custom-call | tf_op jit(solution)/shard_map/pallas_call | solution.py:631
